TPU v7x, 256 devices: a whole 4x4x8 slice. The times are simulated.
256 devices in a mesh: space: 32 (over z, x), tm: 8 (over y, core).
Axes of the slice: x: 4, y: 4, z: 8, core: 2. Of those that a mesh axis runs over, the one named last changes fastest.
Arguments:
- iterate: float32 [8, 240, 23040], P(None, 'tm', 'space'), may hold values from -6 to 6
- residual: float32 [8, 240, 23040], P(None, 'tm', 'space'), may hold values from -24 to 24
- direction: float32 [8, 240, 23040], P(None, 'tm', 'space'), may hold values from -24 to 24
- diffusivity: float32 [23040], P('space'), may hold values from 0.1 to 0.34
- temporal_factor: float32 [240, 240], replicated, may hold values from 0 to 4
- block_tile: int32 [8, 256], P('tm', 'space'), may hold values from -1 to 479, as said below
- footprints: bfloat16 [8, 256, 64, 1440], P('tm', 'space'), may hold values from -0.15625 to 0.15625
- obs_weight: float32 [8, 32, 64], P('tm', 'space'), may hold values from 0.3 to 3
Outputs:
- iterate_next: float32 [8, 240, 23040], P(None, 'tm', 'space')
- residual_next: float32 [8, 240, 23040], P(None, 'tm', 'space')
- direction_next: float32 [8, 240, 23040], P(None, 'tm', 'space')
Inputs may be any that keep to these rules, and one draw needn't show every extreme that they name: `block_tile`: entry -1 marks a padding slot. Tile g belongs to index g // 15 of space. The valid entries of one device name distinct tiles, at most 2 of them of one owner; in each row of tm one owner is named exactly 2 times by every device.
All inputs are finite; a program needn't handle non-finite values.
Results may differ from a plain program's by a relative error of at most 0.017.
Values may be sent and summed in bfloat16 or wider, within the bound.
No kernel may reach another device: no remote copies, remote signals or barrier semaphores. Data moves between devices by JAX's collectives and lax.ppermute only.
A program may use at most 128 MiB of HBM per device.

v0:
```python
import jax
import jax.numpy as jnp
from jax import lax
from jax.sharding import PartitionSpec as P

LON = 720
TC = 48
NB = 8
DIFF = 2


def for_sending(value):

    def short(part):
        return part.astype(jnp.bfloat16) if part.dtype == jnp.float32 else part

    return jax.tree.map(short, value)


def extended_2(cells, sides, width):
    for axis, dim in sides:
        count = lax.axis_size(axis)
        ends = count - 1
        head = lax.slice_in_dim(cells, 0, width, axis=dim)
        tail = lax.slice_in_dim(cells, cells.shape[dim] - width, cells.shape[dim], axis=dim)
        cells = jnp.concatenate(
            [
                lax.ppermute(tail, axis, [(i, (i + 1) % count) for i in range(ends)]),
                cells,
                lax.ppermute(head, axis, [((i + 1) % count, i) for i in range(ends)]),
            ],
            axis=dim,
        )
    return cells


def temporal(field, matrix):
    combined = jnp.einsum(
        "tu,kuc->ktc",
        matrix,
        lax.all_to_all(
            field.astype(jnp.bfloat16), "tm", split_axis=2, concat_axis=1, tiled=True
        ).astype(field.dtype),
        precision=lax.Precision.HIGHEST,
    )
    return lax.all_to_all(
        for_sending(combined), "tm", split_axis=1, concat_axis=2, tiled=True
    ).astype(combined.dtype)


def diffuse(field, conduct):
    samples, window, cell_count = field.shape
    rows_here = cell_count // LON
    for sweep_index in range(DIFF):
        scaled_field = field * conduct
        extended = extended_2(for_sending(scaled_field), (("space", 2),), LON).astype(
            scaled_field.dtype
        )
        planes = extended.reshape(samples, window, rows_here + 2, LON)
        centre = planes[:, :, 1:-1, :]
        laplace = (
            planes[:, :, :-2, :]
            + planes[:, :, 2:, :]
            + jnp.roll(centre, 1, 3)
            + jnp.roll(centre, -1, 3)
            - 4.0 * centre
        )
        field = field + conduct * laplace.reshape(samples, window, cell_count)
    return field


def local(
    iterate, residual, direction, diffusivity, temporal_factor, block_tile, footprints, obs_weight
):
    samples, window, cell_count = direction.shape
    tiles_here = cell_count // TC
    entries = block_tile[0]
    blocks_here = entries.shape[0]
    present = entries >= 0
    mixed = temporal(direction, temporal_factor)
    spread = diffuse(mixed, diffusivity)
    tiled = spread.astype(jnp.bfloat16).reshape(samples, window, tiles_here, TC)
    empty_blocks = jnp.zeros((blocks_here, samples, window * TC), jnp.float32)
    segment = lax.all_gather(tiled, "space", axis=2, tiled=True)
    count_tiles = segment.shape[2]
    selector = (entries[:, None] == jnp.arange(count_tiles)[None, :]).astype(jnp.bfloat16)
    picked = jnp.einsum("bj,ktjc->bktc", selector, segment, preferred_element_type=jnp.float32)
    blocks = picked.reshape(empty_blocks.shape).astype(jnp.bfloat16)
    footprint = footprints[0]
    batches = obs_weight.shape[1]
    slot_obs = jnp.einsum("bmx,bkx->bkm", footprint, blocks, preferred_element_type=jnp.float32)
    batch_obs = jnp.sum(slot_obs.reshape(batches, NB, samples, footprint.shape[1]), axis=1)
    weighted = (obs_weight[0][:, None, :] * batch_obs).astype(jnp.bfloat16)
    grouped = footprint.reshape(batches, NB, footprint.shape[1], footprint.shape[2])
    gradient = jnp.einsum("anmx,akm->ankx", grouped, weighted, preferred_element_type=jnp.float32)
    gradient = gradient.reshape(blocks_here, samples, footprint.shape[2])
    gradient = jnp.where(present[:, None, None], gradient, 0.0).astype(jnp.bfloat16)
    selector = (
        entries[:, None] == jnp.arange(lax.axis_size("space") * tiles_here)[None, :]
    ).astype(jnp.bfloat16)
    summed = lax.psum_scatter(
        jnp.einsum("bj,bkx->jkx", selector, gradient, preferred_element_type=jnp.float32).astype(
            jnp.bfloat16
        ),
        "space",
        scatter_dimension=0,
        tiled=True,
    ).astype(jnp.float32)
    pulled = (
        summed.reshape(tiles_here, samples, window, TC)
        .transpose(1, 2, 0, 3)
        .reshape(samples, window, cell_count)
    )
    back = diffuse(pulled, diffusivity)
    image = direction + temporal(back, temporal_factor.T)
    old_norm, curvature = lax.psum(
        (jnp.sum(residual * residual, axis=(1, 2)), jnp.sum(direction * image, axis=(1, 2))),
        ("space", "tm"),
    )
    step_size = old_norm / curvature
    residual_next = residual - step_size[:, None, None] * image
    new_norm = lax.psum(jnp.sum(residual_next * residual_next, axis=(1, 2)), ("space", "tm"))
    iterate_next = iterate + step_size[:, None, None] * direction
    direction_next = residual_next + (new_norm / old_norm)[:, None, None] * direction
    return (iterate_next, residual_next, direction_next)


def solution(mesh):
    return jax.shard_map(
        local,
        mesh=mesh,
        in_specs=(
            P(None, "tm", "space"),
            P(None, "tm", "space"),
            P(None, "tm", "space"),
            P("space"),
            P(),
            P("tm", "space"),
            P("tm", "space", None, None),
            P("tm", "space", None),
        ),
        out_specs=(P(None, "tm", "space"), P(None, "tm", "space"), P(None, "tm", "space")),
        check_vma=False,
    )
```

profile of v0, /device:TPU:1, one launch (start us, length us, event | category | flops | bytes accessed | tf_op | source)
XLA Modules:
  0.0 833.4 jit_solution(11026537258770947451)
XLA Ops:
  12.0 14.0 %all_to_all.54 = bf16[8,2,10800]{2,1,0:T(2,128)(2,1)} all-to-all(bf16[8,2,10800]{2,1,0:T(2,128)(2,1)S(1)} %reshape.151), channel_id=1, replica_groups=mesh['space'=32,'tm'=8] {'tm'}, dimensions={0} | all-to-all | bytes 691200 | tf_op jit(solution)/shard_map/all_to_all | solution.py:41
  26.0 3.1 reshape.152
  32.1 12.3 %all_to_all.55 = bf16[8,240,90]{2,0,1:T(8,128)(2,1)S(1)} all-to-all(bf16[8,240,90]{2,0,1:T(8,128)(2,1)S(1)} %copy.98), channel_id=1, replica_groups=mesh['space'=32,'tm'=8] {'tm'}, dimensions={1} | all-to-all | bytes 691200 | tf_op jit(solution)/shard_map/all_to_all | solution.py:46
  47.9 3.4 collective-permute-start
  54.9 2.8 collective-permute-done
  57.7 4.6 collective-permute-done.1
  67.5 3.1 collective-permute-start.2
  76.2 3.1 reshape.128
  84.3 3.1 reshape.130
  87.4 4.9 fusion.5
  93.8 215.8 %all-gather.2.cloned.1.call-done = bf16[8,30,480,48]{3,0,1,2:T(8,128)(2,1)} async-done(((bf16[8,30,15,48]{3,0,1,2:T(8,128)(2,1)}), bf16[8,30,480,48]{3,0,1,2:T(8,128)(2,1)}) %all-gather.2.cloned.1.call-update) | async-done | bytes 11059216 | tf_op jit(solution)/shard_map/all_gather | solution.py:84
  309.6 26.4 %fusion.9 = bf16[8,8,30,48]{3,0,2,1:T(8,128)(2,1)S(1)} fusion(bf16[8,30,480,48]{3,0,1,2:T(8,128)(2,1)} %all-gather.2.cloned.1.call-done, s32[8]{0:T(128)S(1)} %bitcast.153), kind=kOutput, calls=%fused_computation.14 | convolution fusion | flops 88569600 | bytes 11243552 | tf_op jit(solution)/shard_map/bj,ktjc->bktc/dot_general | solution.py:87
  338.1 3.7 convolution_convert_fusion
  341.8 20.4 %copy.109 = bf16[480,8,1440]{2,1,0:T(8,128)(2,1)} copy(bf16[480,8,1440]{2,0,1:T(8,128)(2,1)S(1)} %convolution_convert_fusion) | data formatting | bytes 22118400 | tf_op jit(solution)/shard_map/convert_element_type | solution.py:102
  362.2 230.0 %reduce-scatter.2.cloned.1.call-done = bf16[15,8,1440]{2,1,0:T(8,128)(2,1)} async-done(((bf16[480,8,1440]{2,1,0:T(8,128)(2,1)}), bf16[15,8,1440]{2,1,0:T(8,128)(2,1)}) %reduce-scatter.2.cloned.1.call-update) | async-done | bytes 345616 | tf_op jit(solution)/shard_map/reduce_scatter | solution.py:101
  592.2 3.0 reshape.141
  599.5 3.0 collective-permute-start.4
  606.5 4.6 collective-permute-done.5
  618.4 2.9 collective-permute-done.6
  621.4 3.8 collective-permute-done.7
  629.8 19.2 %all_to_all.56 = bf16[8,2,10800]{2,1,0:T(2,128)(2,1)S(1)} all-to-all(bf16[8,2,10800]{2,1,0:T(2,128)(2,1)S(1)} %reshape.153), channel_id=1, replica_groups=mesh['space'=32,'tm'=8] {'tm'}, dimensions={0} | all-to-all | bytes 691200 | tf_op jit(solution)/shard_map/all_to_all | solution.py:41
  652.8 12.3 %all_to_all.57 = bf16[8,240,90]{2,0,1:T(8,128)(2,1)S(1)} all-to-all(bf16[8,240,90]{2,0,1:T(8,128)(2,1)S(1)} %copy.116), channel_id=1, replica_groups=mesh['space'=32,'tm'=8] {'tm'}, dimensions={1} | all-to-all | bytes 691200 | tf_op jit(solution)/shard_map/all_to_all | solution.py:46
  667.8 81.2 %all-reduce = (f32[8]{0:T(128)S(1)}, f32[8]{0:T(128)S(1)}) all-reduce(f32[8]{0:T(128)S(1)} %get-tuple-element.31, f32[8]{0:T(128)S(1)} %get-tuple-element.7), channel_id=1, replica_groups=mesh['space'=32,'tm'=8] {'space','tm'}, use_global_device_ids=true, to_apply=%region_1.2 | all-reduce | flops 16 | bytes 128 | tf_op jit(solution)/shard_map/psum | solution.py:116
  750.5 73.2 %psum.23 = f32[8]{0:T(128)S(1)} all-reduce(f32[8]{0:T(128)S(1)} %get-tuple-element.5), channel_id=1, replica_groups=mesh['space'=32,'tm'=8] {'space','tm'}, use_global_device_ids=true, to_apply=%region_6.7 | all-reduce | flops 8 | bytes 64 | tf_op jit(solution)/shard_map/psum | solution.py:122
  (97 shorter events, 64.7 us)
Async XLA Ops:
  7.2 329.7 %copy-start = (bf16[1,8,64,1440]{3,2,1,0:T(8,128)(2,1)S(1)}, bf16[1,8,64,1440]{3,2,1,0:T(8,128)(2,1)}, u32[]{:S(2)}) copy-start(bf16[1,8,64,1440]{3,2,1,0:T(8,128)(2,1)} %param.14) | copy-start | bytes 4423684
  7.2 302.4 %all-gather.2.cloned.1.call-start = ((), (), s32[]{:S(2)}) async-start(), calls=%async_computation.5 | async-start | bytes 30412800 | tf_op jit(solution)/shard_map/all_gather | solution.py:84
  44.4 1.5 copy-start.11
  47.9 9.9 %collective-permute-start = (bf16[8,30,720]{2,0,1:T(8,128)(2,1)}, bf16[8,30,720]{2,0,1:T(8,128)(2,1)}, u32[]{:S(2)}, u32[]{:S(2)}) collective-permute-start(bf16[8,30,720]{2,0,1:T(8,128)(2,1)} %multiply_convert_fusion.6), channel_id=1, source_target_pairs={{0,8},{8,16},{16,24},{24,32},{32,40},{40,48},{48,56},{56,64},{64,7... | collective-permute-start | bytes 1036808 | tf_op jit(solution)/shard_map/ppermute | solution.py:28
  51.3 11.0 %collective-permute-start.1 = (bf16[8,30,720]{2,0,1:T(8,128)(2,1)}, bf16[8,30,720]{2,0,1:T(8,128)(2,1)}, u32[]{:S(2)}, u32[]{:S(2)}) collective-permute-start(bf16[8,30,720]{2,0,1:T(8,128)(2,1)} %multiply_convert_fusion.6), channel_id=1, source_target_pairs={{8,0},{16,8},{24,16},{32,24},{40,32},{48,40},{56,48},{64,56},{72,6... | collective-permute-start | bytes 1036808 | tf_op jit(solution)/shard_map/ppermute | solution.py:30
  63.6 1.1 copy-start.3
  64.7 2.0 copy-start.6
  65.8 0.9 copy-start.2
  67.5 11.8 %collective-permute-start.2 = (bf16[8,30,720]{2,0,1:T(8,128)(2,1)}, bf16[8,30,720]{2,0,1:T(8,128)(2,1)}, u32[]{:S(2)}, u32[]{:S(2)}) collective-permute-start(bf16[8,30,720]{2,0,1:T(8,128)(2,1)} %fusion.47), channel_id=1, source_target_pairs={{0,8},{8,16},{16,24},{24,32},{32,40},{40,48},{48,56},{56,64},{64,7... | collective-permute-start | bytes 1036808 | tf_op jit(solution)/shard_map/ppermute | solution.py:28
  70.7 9.8 %collective-permute-start.3 = (bf16[8,30,720]{2,0,1:T(8,128)(2,1)}, bf16[8,30,720]{2,0,1:T(8,128)(2,1)}, u32[]{:S(2)}, u32[]{:S(2)}) collective-permute-start(bf16[8,30,720]{2,0,1:T(8,128)(2,1)} %fusion.47), channel_id=1, source_target_pairs={{8,0},{16,8},{24,16},{32,24},{40,32},{48,40},{56,48},{64,56},{72,6... | collective-permute-start | bytes 1036808 | tf_op jit(solution)/shard_map/ppermute | solution.py:30
  92.3 1.4 copy-start.12
  93.5 498.7 %reduce-scatter.2.cloned.1.call-start = ((), (), s32[]{:S(2)}) async-start(), calls=%async_computation.6 | async-start | bytes 12165120 | tf_op jit(solution)/shard_map/reduce_scatter | solution.py:101
  309.6 27.3 %copy-start.13 = (f32[1,1,64]{2,1,0:T(1,128)S(1)}, f32[1,1,64]{2,1,0:T(1,128)}, u32[]{:S(2)}) copy-start(f32[1,1,64]{2,1,0:T(1,128)} %param.15) | copy-start | bytes 772
  599.5 7.0 collective-permute-start.4
  602.5 8.6 %collective-permute-start.5 = (bf16[8,30,720]{2,0,1:T(8,128)(2,1)}, bf16[8,30,720]{2,0,1:T(8,128)(2,1)}, u32[]{:S(2)}, u32[]{:S(2)}) collective-permute-start(bf16[8,30,720]{2,0,1:T(8,128)(2,1)} %multiply_convert_fusion.3), channel_id=1, source_target_pairs={{8,0},{16,8},{24,16},{32,24},{40,32},{48,40},{56,48},{64,56},{72,6... | collective-permute-start | bytes 1036808 | tf_op jit(solution)/shard_map/ppermute | solution.py:30
  604.7 7.7 copy-start.4
  612.5 1.1 copy-start.5
  614.2 7.1 collective-permute-start.6
  616.9 8.3 collective-permute-start.7
  649.0 2.9 copy-start.10
  665.1 1.1 copy-start.7
  665.5 1.2 copy-start.8
  750.5 75.8 %copy-start.9 = (f32[8,30,720]{2,0,1:T(8,128)}, f32[8,30,720]{2,0,1:T(8,128)S(1)}, u32[]{:S(2)}) copy-start(f32[8,30,720]{2,0,1:T(8,128)S(1)} %get-tuple-element.6) | copy-start | bytes 2073604
  823.8 2.6 copy-start.1
Sparse Core Ops, SparseCore 0:
  93.6 215.9 all-gather.1
  362.4 229.8 reduce-scatter.1
where the time goes:
time: 841 us; the launch traced here: 833 us
  waiting for transfers between devices  468 us (56%)
  blocking collectives  212 us (25%)
  local copies, waits for them, and re-layouts  62.5 us (7%)
  matrix products  33.5 us (4%)
  other arithmetic  25.1 us (3%)
  starting transfers between devices  18 us (2%)
  between operations  14.6 us (2%)
    reduce_scatter x1, waiting for transfers between devices, local(): lax.psum_scatter(jnp.einsum('bj,bkx->jkx', selector, gradient, preferred_...  230 us
    all_gather x1, waiting for transfers between devices, local(): segment = lax.all_gather(tiled, 'space', axis=2, tiled=True)  216 us
    psum x1, blocking collectives, local(): lax.psum((jnp.sum(residual * residual, axis=(1, 2)), jnp.sum(direction *...  81.2 us
    psum x1, blocking collectives, local(): lax.psum(jnp.sum(residual_next * residual_next, axis=(1, 2)), ('space', '...  73.2 us
    all_to_all x2, blocking collectives, temporal(): lax.all_to_all(field.astype(jnp.bfloat16), 'tm', split_axis=2, concat_axi...  33.1 us
    dot_general x1, matrix products, local(): jnp.einsum('bj,ktjc->bktc', selector, segment, preferred_element_type=jnp...  26.4 us
    all_to_all x2, blocking collectives, temporal(): lax.all_to_all(for_sending(combined), 'tm', split_axis=1, concat_axis=2,...  24.5 us
    convert_element_type x1, local copies, waits for them, and re-layouts, local(): jnp.einsum('bj,bkx->jkx', selector, gradient, preferred_element_type=jnp....  20.4 us
  transfers between devices with their start and end apart: 10, of which 9 were waited for; matrix products, arithmetic and copies ran while one was open for 1% of the time, Pallas kernels for 0%

commit v1 on v0

--- a/solution.py
+++ b/solution.py
@@ -81,7 +81,9 @@
     spread = diffuse(mixed, diffusivity)
     tiled = spread.astype(jnp.bfloat16).reshape(samples, window, tiles_here, TC)
     empty_blocks = jnp.zeros((blocks_here, samples, window * TC), jnp.float32)
-    segment = lax.all_gather(tiled, "space", axis=2, tiled=True)
+    segment = jnp.concatenate(
+        lax.all_to_all(jnp.stack(lax.axis_size("space") * [tiled], 0), "space", 0, 0), 2
+    )
     count_tiles = segment.shape[2]
     selector = (entries[:, None] == jnp.arange(count_tiles)[None, :]).astype(jnp.bfloat16)
     picked = jnp.einsum("bj,ktjc->bktc", selector, segment, preferred_element_type=jnp.float32)

time: 841 us -> 1050 us (1.25)
  local copies, waits for them, and re-layouts: 62.5 us -> 238 us
  waiting for transfers between devices: 468 us -> 499 us
  matrix products: 33.5 us -> 15.5 us
  starting transfers between devices: 18 us -> 33.1 us
    all_to_all x0 -> x1, waiting for transfers between devices: none -> 235 us  [local(): lax.all_to_all(jnp.stack(lax.axis_size('space') * [tiled], 0), 'space', 0...]
    all_gather x1 -> x0, waiting for transfers between devices: 216 us -> none  [local(): segment = lax.all_gather(tiled, 'space', axis=2, tiled=True)]
    unnamed x32 -> x29, local copies, waits for them, and re-layouts: 12.3 us -> 116 us
    reshape x0 -> x2, local copies, waits for them, and re-layouts: none -> 40.1 us  [local(): jnp.concatenate(lax.all_to_all(jnp.stack(lax.axis_size('space') * [tiled]...]
    dot_general x0 -> x1, local copies, waits for them, and re-layouts: none -> 31.6 us  [local(): jnp.einsum('bj,ktjc->bktc', selector, segment, preferred_element_type=jnp...]
    dot_general x1, matrix products: 26.4 us -> 7.5 us  [local(): jnp.einsum('bj,ktjc->bktc', selector, segment, preferred_element_type=jnp...]
    all_to_all x0 -> x1, starting transfers between devices: none -> 15 us  [local(): lax.all_to_all(jnp.stack(lax.axis_size('space') * [tiled], 0), 'space', 0...]
    reduce_scatter x1, waiting for transfers between devices: 230 us -> 244 us  [local(): lax.psum_scatter(jnp.einsum('bj,bkx->jkx', selector, gradient, preferred_...]
  transfers between devices with their start and end apart: 10 -> 10, of which waited for: 9 -> 8; matrix products, arithmetic and copies ran while one was open for 1% -> 1% of each run, Pallas kernels for 0% -> 0%
where the time goes in v1:
time: 1050 us; the launch traced here: 1040 us
  waiting for transfers between devices  499 us (48%)
  local copies, waits for them, and re-layouts  238 us (23%)
  blocking collectives  212 us (20%)
  starting transfers between devices  33.1 us (3%)
  other arithmetic  29.5 us (3%)
  matrix products  15.5 us (1%)
  between operations  14.6 us (1%)
    reduce_scatter x1, waiting for transfers between devices, local(): lax.psum_scatter(jnp.einsum('bj,bkx->jkx', selector, gradient, preferred_...  244 us
    all_to_all x1, waiting for transfers between devices, local(): lax.all_to_all(jnp.stack(lax.axis_size('space') * [tiled], 0), 'space', 0...  235 us
    unnamed x29, local copies, waits for them, and re-layouts  116 us
    psum x1, blocking collectives, local(): lax.psum((jnp.sum(residual * residual, axis=(1, 2)), jnp.sum(direction *...  81.2 us
    psum x1, blocking collectives, local(): lax.psum(jnp.sum(residual_next * residual_next, axis=(1, 2)), ('space', '...  73.2 us
    reshape x2, local copies, waits for them, and re-layouts, local(): jnp.concatenate(lax.all_to_all(jnp.stack(lax.axis_size('space') * [tiled]...  40.1 us
    all_to_all x2, blocking collectives, temporal(): lax.all_to_all(field.astype(jnp.bfloat16), 'tm', split_axis=2, concat_axi...  33.2 us
    dot_general x1, local copies, waits for them, and re-layouts, local(): jnp.einsum('bj,ktjc->bktc', selector, segment, preferred_element_type=jnp...  31.6 us
  transfers between devices with their start and end apart: 10, of which 8 were waited for; matrix products, arithmetic and copies ran while one was open for 1% of the time, Pallas kernels for 0%

profile of v1, /device:TPU:1, one launch (start us, length us, event | category | flops | bytes accessed | tf_op | source)
XLA Modules:
  0.0 1042.3 jit_solution(13317096539624262060)
XLA Ops:
  12.0 14.0 %all_to_all.59 = bf16[8,2,10800]{2,1,0:T(2,128)(2,1)} all-to-all(bf16[8,2,10800]{2,1,0:T(2,128)(2,1)S(1)} %reshape.161), channel_id=1, replica_groups=mesh['space'=32,'tm'=8] {'tm'}, dimensions={0} | all-to-all | bytes 691200 | tf_op jit(solution)/shard_map/all_to_all | solution.py:41
  32.1 12.3 %all_to_all.60 = bf16[8,240,90]{2,0,1:T(8,128)(2,1)S(1)} all-to-all(bf16[8,240,90]{2,0,1:T(8,128)(2,1)S(1)} %copy.99), channel_id=1, replica_groups=mesh['space'=32,'tm'=8] {'tm'}, dimensions={1} | all-to-all | bytes 691200 | tf_op jit(solution)/shard_map/all_to_all | solution.py:46
  47.8 3.4 collective-permute-start
  57.7 4.6 collective-permute-done.1
  87.3 4.9 fusion.3
  92.3 10.0 broadcast_bitcast_fusion
  102.3 50.2 %reshape.163 = bf16[32,2,86400]{2,1,0:T(2,128)(2,1)} reshape(bf16[32,30,15,8,48]{4,3,2,1,0:T(8,128)(2,1)} %broadcast_bitcast_fusion) | data formatting | bytes 22118400
  152.5 15.0 %all-to-all-start.2 = ((bf16[32,2,86400]{2,1,0:T(2,128)(2,1)}), bf16[32,2,86400]{2,1,0:T(2,128)(2,1)}, u32[]{:S(2)}, u32[]{:S(2)}) async-start(bf16[32,2,86400]{2,1,0:T(2,128)(2,1)} %reshape.163), calls=%async_computation.2 | async-start | bytes 22118400 | tf_op jit(solution)/shard_map/all_to_all | solution.py:85
  167.8 235.5 %all-to-all-done.2 = bf16[32,2,86400]{2,1,0:T(2,128)(2,1)} async-done(((bf16[32,2,86400]{2,1,0:T(2,128)(2,1)}), bf16[32,2,86400]{2,1,0:T(2,128)(2,1)}, u32[]{:S(2)}, u32[]{:S(2)}) %all-to-all-start.2) | async-done | bytes 11059232 | tf_op jit(solution)/shard_map/all_to_all | solution.py:85
  403.2 42.2 %reshape.164 = bf16[32,30,15,8,48]{4,3,2,1,0:T(8,128)(2,1)} reshape(bf16[32,2,86400]{2,1,0:T(2,128)(2,1)} %all-to-all-done.2) | data formatting | bytes 22118400
  445.5 20.5 %bitcast_bitcast_fusion = bf16[8,30,32,15,48]{4,0,3,1,2:T(8,128)(2,1)} fusion(bf16[32,30,15,8,48]{4,3,2,1,0:T(8,128)(2,1)} %reshape.164), kind=kLoop, calls=%fused_computation.94 | loop fusion | bytes 22118400 | tf_op jit(solution)/shard_map/reshape | solution.py:84
  466.0 19.6 %copy.106 = bf16[8,30,32,15,48]{4,0,3,2,1:T(8,128)(2,1)} copy(bf16[8,30,32,15,48]{4,0,3,1,2:T(8,128)(2,1)} %bitcast_bitcast_fusion) | data formatting | bytes 22118400 | tf_op jit(solution)/shard_map/reshape | solution.py:84
  485.6 31.6 %copy.107 = bf16[8,30,48,480]{3,2,1,0:T(8,128)(2,1)} copy(bf16[8,30,48,480]{2,0,3,1:T(8,128)(2,1)} %bitcast.146) | data formatting | bytes 22118400 | tf_op jit(solution)/shard_map/bj,ktjc->bktc/dot_general | solution.py:89
  517.2 7.5 convolution_convert_fusion.1
  525.9 3.7 convolution_convert_fusion
  529.6 20.4 %copy.110 = bf16[480,8,1440]{2,1,0:T(8,128)(2,1)} copy(bf16[480,8,1440]{2,0,1:T(8,128)(2,1)S(1)} %convolution_convert_fusion) | data formatting | bytes 22118400 | tf_op jit(solution)/shard_map/convert_element_type | solution.py:104
  550.1 243.6 %reduce-scatter.2.cloned.1.call-done = bf16[15,8,1440]{2,1,0:T(8,128)(2,1)} async-done(((bf16[480,8,1440]{2,1,0:T(8,128)(2,1)}), bf16[15,8,1440]{2,1,0:T(8,128)(2,1)}) %reduce-scatter.2.cloned.1.call-update) | async-done | bytes 345616 | tf_op jit(solution)/shard_map/reduce_scatter | solution.py:103
  793.7 3.2 reshape.152
  810.4 4.4 collective-permute-done.5
  825.4 3.8 collective-permute-done.7
  833.8 19.3 %all_to_all.61 = bf16[8,2,10800]{2,1,0:T(2,128)(2,1)} all-to-all(bf16[8,2,10800]{2,1,0:T(2,128)(2,1)S(1)} %reshape.165), channel_id=1, replica_groups=mesh['space'=32,'tm'=8] {'tm'}, dimensions={0} | all-to-all | bytes 691200 | tf_op jit(solution)/shard_map/all_to_all | solution.py:41
  859.2 12.5 %all_to_all.62 = bf16[8,240,90]{2,0,1:T(8,128)(2,1)S(1)} all-to-all(bf16[8,240,90]{2,0,1:T(8,128)(2,1)S(1)} %copy.117), channel_id=1, replica_groups=mesh['space'=32,'tm'=8] {'tm'}, dimensions={1} | all-to-all | bytes 691200 | tf_op jit(solution)/shard_map/all_to_all | solution.py:46
  875.8 81.2 %all-reduce = (f32[8]{0:T(128)S(1)}, f32[8]{0:T(128)S(1)}) all-reduce(f32[8]{0:T(128)S(1)} %get-tuple-element.31, f32[8]{0:T(128)S(1)} %get-tuple-element.7), channel_id=1, replica_groups=mesh['space'=32,'tm'=8] {'space','tm'}, use_global_device_ids=true, to_apply=%region_1.2 | all-reduce | flops 16 | bytes 128 | tf_op jit(solution)/shard_map/psum | solution.py:118
  959.3 73.2 %psum.23 = f32[8]{0:T(128)S(1)} all-reduce(f32[8]{0:T(128)S(1)} %get-tuple-element.5), channel_id=1, replica_groups=mesh['space'=32,'tm'=8] {'space','tm'}, use_global_device_ids=true, to_apply=%region_6.7 | all-reduce | flops 8 | bytes 64 | tf_op jit(solution)/shard_map/psum | solution.py:124
  (93 shorter events, 90.9 us)
Async XLA Ops:
  7.2 517.5 %copy-start = (bf16[1,8,64,1440]{3,2,1,0:T(8,128)(2,1)S(1)}, bf16[1,8,64,1440]{3,2,1,0:T(8,128)(2,1)}, u32[]{:S(2)}) copy-start(bf16[1,8,64,1440]{3,2,1,0:T(8,128)(2,1)} %param.14) | copy-start | bytes 4423684
  44.4 1.5 copy-start.8
  47.8 9.9 collective-permute-start
  51.2 11.0 %collective-permute-start.1 = (bf16[8,30,720]{2,0,1:T(8,128)(2,1)}, bf16[8,30,720]{2,0,1:T(8,128)(2,1)}, u32[]{:S(2)}, u32[]{:S(2)}) collective-permute-start(bf16[8,30,720]{2,0,1:T(8,128)(2,1)} %multiply_convert_fusion.6), channel_id=1, source_target_pairs={{8,0},{16,8},{24,16},{32,24},{40,32},{48,40},{56,48},{64,56},{72,6... | collective-permute-start | bytes 1036808 | tf_op jit(solution)/shard_map/ppermute | solution.py:30
  63.5 1.1 copy-start.3
  64.6 2.0 copy-start.5
  65.8 0.9 copy-start.2
  67.5 12.1 %collective-permute-start.2 = (bf16[8,30,720]{2,0,1:T(8,128)(2,1)}, bf16[8,30,720]{2,0,1:T(8,128)(2,1)}, u32[]{:S(2)}, u32[]{:S(2)}) collective-permute-start(bf16[8,30,720]{2,0,1:T(8,128)(2,1)} %fusion.42), channel_id=1, source_target_pairs={{0,8},{8,16},{16,24},{24,32},{32,40},{40,48},{48,56},{56,64},{64,7... | collective-permute-start | bytes 1036808 | tf_op jit(solution)/shard_map/ppermute | solution.py:28
  70.6 9.8 collective-permute-start.3
  152.5 15.2 %copy-start.9 = (s32[1,8]{1,0:T(1,128)S(1)}, s32[1,8]{1,0:T(1,128)}, u32[]{:S(2)}) copy-start(s32[1,8]{1,0:T(1,128)} %param.13) | copy-start | bytes 100
  152.5 250.7 %all-to-all-start.2 = ((bf16[32,2,86400]{2,1,0:T(2,128)(2,1)}), bf16[32,2,86400]{2,1,0:T(2,128)(2,1)}, u32[]{:S(2)}, u32[]{:S(2)}) async-start(bf16[32,2,86400]{2,1,0:T(2,128)(2,1)} %reshape.163), calls=%async_computation.2 | async-start | bytes 22118400 | tf_op jit(solution)/shard_map/all_to_all | solution.py:85
  167.5 626.2 %reduce-scatter.2.cloned.1.call-start = ((), (), s32[]{:S(2)}) async-start(), calls=%async_computation.6 | async-start | bytes 12165120 | tf_op jit(solution)/shard_map/reduce_scatter | solution.py:103
  517.2 7.5 copy-start.10
  803.1 7.2 collective-permute-start.4
  806.2 8.6 collective-permute-start.5
  816.1 1.1 copy-start.4
  817.2 1.1 copy-start.1
  818.4 7.0 collective-permute-start.6
  821.0 8.3 collective-permute-start.7
  871.8 1.5 copy-start.6
  873.3 83.8 %copy-start.7 = (f32[8,30,720]{2,0,1:T(8,128)S(1)}, f32[8,30,720]{2,0,1:T(8,128)}, u32[]{:S(2)}) copy-start(f32[8,30,720]{2,0,1:T(8,128)} %param.9) | copy-start | bytes 2073604
Sparse Core Ops, SparseCore 0:
  550.2 243.4 reduce-scatter.1
